TPU v7x, 256 devices: a whole 4x4x8 slice. The times are simulated.
256 devices in a mesh: section: 4 (over x), dp: 4 (over y), chan: 16 (over z, core).
Axes of the slice: x: 4, y: 4, z: 8, core: 2. Of those that a mesh axis runs over, the one named last changes fastest.
Arguments:
- feats: bfloat16 [8, 32, 128, 2048], P('dp', None, None, 'chan'), may hold values from -6 to 6
- offsets: int32 [8], P('dp'), may hold values from 0 to 127
- widths: int32 [8], P('dp'), may hold values from 32 to 64
- labels: int32 [8, 32, 128], P('dp'), may hold values from 0 to 19
- dw_kernel: bfloat16 [4, 9, 2048], P('section', None, 'chan'), may hold values from -2 to 2
- pw_weight: bfloat16 [4, 2048, 256], P('section', 'chan'), may hold values from -0.125 to 0.125
- pw_bias: float32 [4, 256], P('section', 'chan'), may hold values from -3 to 3
- proj: bfloat16 [4, 256, 256], P('section', 'chan'), may hold values from -0.1875 to 0.1875
- proj_bias: float32 [256], P('chan'), may hold values from -3 to 3
- upstream: bfloat16 [256, 8, 32, 128], P('chan', 'dp'), may hold values from -6 to 6
Outputs:
- aspp_out: bfloat16 [256, 8, 32, 128], P('chan', 'dp')
- input_grad: bfloat16 [8, 32, 128, 2048], P('dp', 'section', None, 'chan')
- grad_dw: float32 [4, 9, 2048], P('section', None, 'chan')
- grad_pw: float32 [4, 2048, 256], P('section', 'chan')
- grad_pw_bias: float32 [4, 256], P('section', 'chan')
- grad_proj: float32 [4, 256, 256], P('section', 'chan')
- grad_proj_bias: float32 [256], P('chan')
All inputs are finite; a program needn't handle non-finite values.
Results may differ from a plain program's by a relative error of at most 0.008.
Values may be sent and summed in bfloat16 or wider, within the bound.
No kernel may reach another device: no remote copies, remote signals or barrier semaphores. Data moves between devices by JAX's collectives and lax.ppermute only.
A program may use at most 128 MiB of HBM per device.

v0:
```python
import math
import jax
import jax.numpy as jnp
from jax import lax
from jax.sharding import PartitionSpec as P

RATE = 6
void_class = 19


def prefix(shard, axis, combine, identity):
    devices, place = (lax.axis_size(axis), lax.axis_index(axis))
    everything = lax.all_gather(shard, axis)
    start = jnp.broadcast_to(jnp.asarray(identity, shard.dtype), shard.shape)

    def step(k, before):
        reached = k < place
        new = combine(before, everything[k])
        return jnp.where(reached, new, before)

    return lax.fori_loop(0, devices, step, start)


def spread(value, axis, source):
    kept = jnp.where(lax.axis_index(axis) == source, value, 0).astype(value.dtype)
    return lax.psum(kept, axis)


def column_band(offsets, widths, col_count):
    columns = jnp.arange(col_count, dtype=jnp.int32)
    return jnp.mod(columns[None, :] - offsets[:, None], col_count) < widths[:, None]


def swish_slope(value):
    sig = jax.nn.sigmoid(value)
    return sig * (1.0 + value * (1.0 - sig))


def add_terms(earlier, latter):
    return earlier + latter


def local(feats, offsets, widths, labels, dw_kernel, pw_weight, pw_bias, proj, proj_bias, upstream):
    frame_count, row_count, col_count, chan_count = feats.shape
    segments = lax.axis_size("section")
    dilation = RATE * lax.axis_index("section")
    margin = RATE * (segments - 1)
    keep = column_band(offsets, widths, col_count)
    masked = feats * keep[:, None, :, None].astype(jnp.bfloat16)
    padded = jnp.pad(masked, ((0, 0), (margin, margin), (margin, margin), (0, 0)))
    kernel = dw_kernel[0].astype(jnp.float32)
    pixel_count = frame_count * row_count * col_count
    scaling = 1.0 / math.sqrt(pixel_count * lax.axis_size("dp"))

    def tap_slice(source, tap_index, direction):
        row_step = tap_index // 3 - 1
        col_step = tap_index % 3 - 1
        anchor = (
            0,
            margin + direction * dilation * row_step,
            margin + direction * dilation * col_step,
            0,
        )
        return lax.dynamic_slice(source, anchor, (frame_count, row_count, col_count, chan_count))

    accum = jnp.zeros((frame_count, row_count, col_count, chan_count), jnp.float32)
    for tap_index in range(9):
        accum = accum + tap_slice(padded, tap_index, 1).astype(jnp.float32) * kernel[tap_index]
    depth_out = accum.astype(jnp.bfloat16)
    depth_rows = depth_out.reshape(pixel_count, chan_count)
    weight = pw_weight[0]
    branch_share = pw_bias.shape[1]
    columns = weight
    preact = (
        lax.psum_scatter(
            lax.dot_general(
                columns, depth_rows, (((0,), (1,)), ((), ())), preferred_element_type=jnp.float32
            ),
            "chan",
            scatter_dimension=0,
            tiled=True,
        )
        + pw_bias[0][:, None]
    )
    branch_act = jax.nn.silu(preact).astype(jnp.bfloat16)
    proj_local = proj[0]
    columns = proj_local
    zpart = lax.psum_scatter(
        lax.dot_general(
            columns, branch_act, (((0,), (0,)), ((), ())), preferred_element_type=jnp.float32
        ),
        "chan",
        scatter_dimension=0,
        tiled=True,
    )
    up_rows = upstream.reshape(branch_share, pixel_count).astype(jnp.float32)
    labeled = (labels != void_class).reshape(pixel_count).astype(jnp.float32)
    before = prefix(zpart, "section", add_terms, jnp.zeros_like(zpart))
    zvalue = before + zpart + proj_bias[:, None]
    result = jax.nn.silu(zvalue).astype(jnp.bfloat16)
    gradient = (up_rows * swish_slope(zvalue) * labeled[None, :]).astype(jnp.bfloat16)
    result, out_grad = (result, gradient)
    result, out_grad = (
        spread(result, "section", segments - 1),
        spread(out_grad, "section", segments - 1),
    )
    proj_bias_grad = jnp.sum(out_grad.astype(jnp.float32), axis=1) * scaling
    shard_rows = lax.all_gather(out_grad, "chan", axis=0, tiled=True)
    act_grad = jnp.dot(proj_local, shard_rows, preferred_element_type=jnp.float32)
    piece_grad = lax.dot_general(
        branch_act, shard_rows, (((1,), (1,)), ((), ())), preferred_element_type=jnp.float32
    )
    proj_grad = piece_grad
    act_grad, proj_grad = (act_grad, proj_grad)
    pre_grad = (act_grad * swish_slope(preact)).astype(jnp.bfloat16)
    pw_bias_grad = jnp.sum(pre_grad.astype(jnp.float32), axis=1) * scaling
    shard_rows = lax.all_gather(pre_grad, "chan", axis=0, tiled=True)
    columns = weight
    depth_acc = lax.dot_general(
        shard_rows, columns, (((0,), (1,)), ((), ())), preferred_element_type=jnp.float32
    )
    piece_grad = lax.dot_general(
        depth_rows, shard_rows, (((0,), (1,)), ((), ())), preferred_element_type=jnp.float32
    )
    weight_grad = piece_grad
    depth_acc, weight_grad = (depth_acc, weight_grad)
    depth_grad = depth_acc.astype(jnp.bfloat16).reshape(
        frame_count, row_count, col_count, chan_count
    )
    padded_grad = jnp.pad(depth_grad, ((0, 0), (margin, margin), (margin, margin), (0, 0)))
    depth_f = depth_grad.astype(jnp.float32)
    input_term = jnp.zeros((frame_count, row_count, col_count, chan_count), jnp.float32)
    tap_grads = []
    for tap_index in range(9):
        source = tap_slice(padded, tap_index, 1).astype(jnp.float32)
        tap_grads.append(jnp.sum(source * depth_f, axis=(0, 1, 2)) * scaling)
        input_term = (
            input_term
            + tap_slice(padded_grad, tap_index, -1).astype(jnp.float32) * kernel[tap_index]
        )
    kernel_grad = jnp.stack(tap_grads)
    input_rows = lax.psum_scatter(input_term, "section", scatter_dimension=1, tiled=True)
    input_grad = (input_rows * keep[:, None, :, None].astype(jnp.float32)).astype(jnp.bfloat16)
    kernel_grad, weight_grad, pw_bias_grad, proj_grad, proj_bias_grad = lax.psum(
        (kernel_grad, weight_grad * scaling, pw_bias_grad, proj_grad * scaling, proj_bias_grad),
        "dp",
    )
    aspp_out = result.reshape(branch_share, frame_count, row_count, col_count)
    return (
        aspp_out,
        input_grad,
        kernel_grad[None],
        weight_grad[None],
        pw_bias_grad[None],
        proj_grad[None],
        proj_bias_grad,
    )


def solution(mesh):
    in_specs = (
        P("dp", None, None, "chan"),
        P("dp"),
        P("dp"),
        P("dp", None, None),
        P("section", None, "chan"),
        P("section", "chan", None),
        P("section", "chan"),
        P("section", "chan", None),
        P("chan"),
        P("chan", "dp", None, None),
    )
    out_specs = (
        P("chan", "dp", None, None),
        P("dp", "section", None, "chan"),
        P("section", None, "chan"),
        P("section", "chan", None),
        P("section", "chan"),
        P("section", "chan", None),
        P("chan"),
    )
    return jax.shard_map(local, mesh=mesh, in_specs=in_specs, out_specs=out_specs, check_vma=False)
```

profile of v0, /device:TPU:2, one launch (start us, length us, event | category | flops | bytes accessed | tf_op | source)
XLA Modules:
  0.0 520.5 jit_solution(6234613447369685872)
XLA Ops:
  7.2 0.0 copy-start
  7.2 0.0 reduce-scatter.11.cloned.1.call-start
  7.2 0.7 convert_element_type.135
  7.9 0.7 fusion.36
  8.7 1.8 broadcast_multiply_fusion
  10.5 0.0 copy-start.1
  10.5 1.3 copy-done.1
  11.8 16.0 %fusion.10 = bf16[2,32,128,128]{3,2,1,0:T(8,128)(2,1)S(1)} fusion(bf16[2,32,128,128]{3,2,1,0:T(8,128)(2,1)S(1)} %broadcast_multiply_fusion, f32[128]{0:T(128)S(1)} %get-tuple-element.153, f32[128]{0:T(128)S(1)} %get-tuple-element.154, f32[128]{0:T(128)S(1)} %get-tuple-element.155, f32[128]{0:T(128)S(1)} %get-tuple-element.156, ...), kind=kLoop, calls=%fused_computation.50 | loop fusion | flops 28311552 | bytes 4198928 | tf_op jit(solution)/shard_map/convert_element_type | solution.py:69
  27.8 0.0 copy-done
  27.8 4.5 convolution_bitcast_fusion.1
  32.3 8.9 %copy.33 = f32[256,8192]{1,0:T(8,128)} copy(f32[256,8192]{0,1:T(8,128)} %convolution_bitcast_fusion.1) | data formatting | bytes 16777216
  41.2 0.0 reduce-scatter.11.cloned.1.call-update
  41.2 0.2 reduce-scatter.13.cloned.1.call-start
  41.5 73.4 %reduce-scatter.11.cloned.1.call-done = f32[16,8192]{1,0:T(8,128)} async-done(((f32[256,8192]{1,0:T(8,128)}), f32[16,8192]{1,0:T(8,128)}) %reduce-scatter.11.cloned.1.call-update) | async-done | bytes 524304 | tf_op jit(solution)/shard_map/reduce_scatter | solution.py:75
  114.9 0.0 copy-done.7
  114.9 0.0 copy-done.8
  114.9 5.6 %convolution_bitcast_fusion = f32[256,8192]{0,1:T(8,128)} fusion(bf16[1,16,256]{2,1,0:T(8,128)(2,1)S(1)} %copy-done.7, f32[16,8192]{1,0:T(8,128)} %reduce-scatter.11.cloned.1.call-done, f32[16]{0:T(128)S(1)} %bitcast.133), kind=kOutput, calls=%fused_computation.27 | convolution fusion | flops 67895296 | bytes 8921152 | tf_op jit(solution)/shard_map/dot_general | solution.py:89
  120.6 8.9 %copy.35 = f32[256,8192]{1,0:T(8,128)} copy(f32[256,8192]{0,1:T(8,128)} %convolution_bitcast_fusion) | data formatting | bytes 16777216
  129.5 0.0 reduce-scatter.13.cloned.1.call-update
  129.5 0.0 all-gather.9.cloned.1.call-start
  129.6 69.4 %reduce-scatter.13.cloned.1.call-done = f32[16,8192]{1,0:T(8,128)} async-done(((f32[256,8192]{1,0:T(8,128)}), f32[16,8192]{1,0:T(8,128)}) %reduce-scatter.13.cloned.1.call-update) | async-done | bytes 524304 | tf_op jit(solution)/shard_map/reduce_scatter | solution.py:88
  198.9 0.0 all-gather.9.cloned.1.call-update
  199.0 0.0 all-reduce.9.cloned.1.call-start
  199.0 0.0 copy-done.4
  199.0 0.8 convert.2
  199.9 0.0 copy-done.6
  199.9 32.1 %all-gather.9.cloned.1.call-done = f32[64,8192]{1,0:T(8,128)} async-done(((f32[16,8192]{1,0:T(8,128)}), f32[64,8192]{1,0:T(8,128)}) %all-gather.9.cloned.1.call-update) | async-done | bytes 2097168 | tf_op jit(solution)/shard_map/all_gather | solution.py:13
  232.0 4.9 while.14
  232.0 1.3 add_select_fusion.2
  233.3 1.2 add_select_fusion.2
  234.5 1.2 add_select_fusion.2
  235.7 1.2 add_select_fusion.2
  236.9 2.4 broadcast_select_fusion
  239.3 0.8 copy.39
  240.1 0.0 all-reduce.9.cloned.1.call-update
  240.1 0.0 all-gather.5.cloned.1.call-start
  240.2 48.3 %all-reduce.9.cloned.1.call-done = (bf16[16,2,32,128]{3,2,1,0:T(8,128)(2,1)}, bf16[16,8192]{1,0:T(8,128)(2,1)}) async-done(((bf16[16,2,32,128]{3,2,1,0:T(8,128)(2,1)}, bf16[16,8192]{1,0:T(8,128)(2,1)}), (bf16[16,2,32,128]{3,2,1,0:T(8,128)(2,1)}, bf16[16,8192]{1,0:T(8,128)(2,1)})) %all-reduce.9.cloned.1.call-update) | async-done | bytes 524304 | tf_op jit(solution)/shard_map/psum | solution.py:26
  288.4 0.0 all-gather.5.cloned.1.call-update
  288.5 0.0 all-gather.7.cloned.1.call-start
  288.5 45.4 %all-gather.5.cloned.1.call-done = bf16[256,8192]{1,0:T(8,128)(2,1)} async-done(((bf16[16,8192]{1,0:T(8,128)(2,1)}), bf16[256,8192]{1,0:T(8,128)(2,1)}) %all-gather.5.cloned.1.call-update) | async-done | bytes 4194320 | tf_op jit(solution)/shard_map/all_gather | solution.py:108
  333.9 3.7 convert_reduce_fusion.1
  337.6 0.0 all-gather.7.cloned.1.call-update
  337.6 0.0 reduce-scatter.15.cloned.1.call-start
  337.6 40.8 %all-gather.7.cloned.1.call-done = bf16[256,8192]{1,0:T(8,128)(2,1)} async-done(((bf16[16,8192]{1,0:T(8,128)(2,1)}), bf16[256,8192]{1,0:T(8,128)(2,1)}) %all-gather.7.cloned.1.call-update) | async-done | bytes 4194320 | tf_op jit(solution)/shard_map/all_gather | solution.py:117
  378.4 16.1 %fusion.24 = (f32[128]{0:T(128)S(1)}, f32[128]{0:T(128)S(1)}, f32[128]{0:T(128)S(1)}, f32[128]{0:T(128)S(1)}, f32[128]{0:T(128)S(1)}, /*index=5*/f32[128]{0:T(12...) fusion(s32[]{:T(128)S(6)} %select_n.96, s32[]{:T(128)S(6)} %select_n.95, ...), kind=kOutput, calls=%fused_computation.64 | convolution fusion | flops 567278464 | bytes 8458768 | tf_op jit(solution)/shard_map/dot_general | solution.py:119
  394.5 16.2 %fusion.15 = f32[2,32,128,128]{3,2,1,0:T(8,128)S(1)} fusion(bf16[2,32,128,128]{3,2,1,0:T(8,128)(2,1)S(1)} %bitcast.127, s32[]{:T(128)S(6)} %select_n.96, s32[]{:T(128)S(6)} %select_n.95, s32[]{:T(128)S(6)} %select_n.94, s32[]{:T(128)S(6)} %select_n.93, f32[128]{0:T(128)S(1)} %get-tuple-element.153, f32[128]{0:T(128)S(1)} %get-tuple-element.154, ...), kind=kLoop, calls=%fused_computation.55 | loop fusion | flops 27262976 | bytes 6296080 | tf_op jit(solution)/shard_map/add | solution.py:138
  410.7 0.3 copy.37
  411.0 4.4 copy.50
  415.4 0.0 reduce-scatter.15.cloned.1.call-update
  415.4 0.3 all-reduce.7.cloned.1.call-start
  415.7 0.6 copy-done.3
  416.3 0.2 convert_reduce_fusion
  416.5 3.4 fusion.26
  420.0 17.6 %all-reduce.2 = (f32[1,9,128]{2,1,0:T(8,128)S(1)}, f32[1,16]{1,0:T(1,128)}, f32[1,16,256]{2,1,0:T(8,128)}, f32[16]{0:T(128)}) all-reduce(f32[1,9,128]{2,1,0:T(8,128)S(1)} %bitcast.132, f32[1,16]{1,0:T(1,128)S(1)} %multiply_bitcast_fusion, f32[1,16,256]{2,1,0:T(8,128)S(1)} %fusion.26, ...), channel_id=1, replica_groups=mesh['section'=4,'dp'=4,'chan'=16] {'dp'}, use_global_device_ids=true, to_apply=%region_16.17 | all-reduce | flops 5280 | bytes 42240 | tf_op jit(solution)/shard_map/psum | solution.py:144
  437.7 0.6 copy.32
  438.3 4.5 fusion.25
  442.8 0.0 all-reduce.7.cloned.1.call-update
  442.8 18.3 %reduce-scatter.15.cloned.1.call-done = f32[8,32768]{1,0:T(8,128)} async-done(((f32[32,32768]{1,0:T(8,128)}), f32[8,32768]{1,0:T(8,128)}) %reduce-scatter.15.cloned.1.call-update) | async-done | bytes 1048592
  461.1 1.4 copy.42
  462.5 1.0 fusion.27
  463.5 47.9 %all-reduce.7.cloned.1.call-done = f32[1,128,256]{2,1,0:T(8,128)} async-done(((f32[1,128,256]{2,1,0:T(8,128)}), f32[1,128,256]{2,1,0:T(8,128)}) %all-reduce.7.cloned.1.call-update) | async-done | bytes 131088 | tf_op jit(solution)/shard_map/psum | solution.py:144
  511.3 0.0 copy-done.5
  511.4 0.7 copy.60
  512.1 1.6 copy.61
  (21 shorter events, 0.1 us)
Async XLA Ops:
  7.2 20.7 %copy-start = (bf16[1,128,256]{2,1,0:T(8,128)(2,1)S(1)}, bf16[1,128,256]{2,1,0:T(8,128)(2,1)}, u32[]{:S(2)}) copy-start(bf16[1,128,256]{2,1,0:T(8,128)(2,1)} %param.17) | copy-start | bytes 196612
  7.2 107.7 %reduce-scatter.11.cloned.1.call-start = ((), (), s32[]{:S(2)}) async-start(), calls=%async_computation.7 | async-start | bytes 8912896 | tf_op jit(solution)/shard_map/reduce_scatter | solution.py:75
  10.5 1.4 copy-start.1
  41.2 73.7 %copy-start.7 = (bf16[1,16,256]{2,1,0:T(8,128)(2,1)S(1)}, bf16[1,16,256]{2,1,0:T(8,128)(2,1)}, u32[]{:S(2)}) copy-start(bf16[1,16,256]{2,1,0:T(8,128)(2,1)} %param.19) | copy-start | bytes 24580
  41.2 73.7 %copy-start.8 = (f32[1,16]{1,0:T(1,128)S(1)}, f32[1,16]{1,0:T(1,128)}, u32[]{:S(2)}) copy-start(f32[1,16]{1,0:T(1,128)} %param.18) | copy-start | bytes 196
  41.2 157.7 %reduce-scatter.13.cloned.1.call-start = ((), (), s32[]{:S(2)}) async-start(), calls=%async_computation.8 | async-start | bytes 8912896 | tf_op jit(solution)/shard_map/reduce_scatter | solution.py:88
  129.5 69.5 %copy-start.4 = (bf16[16,2,32,128]{3,2,1,0:T(8,128)(2,1)S(1)}, bf16[16,2,32,128]{3,2,1,0:T(8,128)(2,1)}, u32[]{:S(2)}) copy-start(bf16[16,2,32,128]{3,2,1,0:T(8,128)(2,1)} %param.21) | copy-start | bytes 786436
  129.5 70.4 %copy-start.6 = (s32[2,32,128]{2,1,0:T(8,128)S(1)}, s32[2,32,128]{2,1,0:T(8,128)}, u32[]{:S(2)}) copy-start(s32[2,32,128]{2,1,0:T(8,128)} %param.15) | copy-start | bytes 98308
  129.5 102.5 %all-gather.9.cloned.1.call-start = ((), (), s32[]{:S(2)}) async-start(), calls=%async_computation.6 | async-start | bytes 2621440 | tf_op jit(solution)/shard_map/all_gather | solution.py:13
  199.0 89.5 %all-reduce.9.cloned.1.call-start = ((), (), s32[]{:S(2)}) async-start(), calls=%async_computation.10 | async-start | bytes 1048576 | tf_op jit(solution)/shard_map/psum | solution.py:26
  199.9 37.0 %copy-start.9 = (f32[16]{0:T(128)S(1)}, f32[16]{0:T(128)}, u32[]{:S(2)}) copy-start(f32[16]{0:T(128)} %param.20) | copy-start | bytes 196
  232.0 101.9 %copy-start.2 = (f32[16,8192]{1,0:T(8,128)S(1)}, f32[16,8192]{1,0:T(8,128)}, u32[]{:S(2)}) copy-start(f32[16,8192]{1,0:T(8,128)} %reduce-scatter.11.cloned.1.call-done) | copy-start | bytes 1572868
  240.1 93.8 %all-gather.5.cloned.1.call-start = ((), (), s32[]{:S(2)}) async-start(), calls=%async_computation.3 | async-start | bytes 4456448 | tf_op jit(solution)/shard_map/all_gather | solution.py:108
  288.5 90.0 %all-gather.7.cloned.1.call-start = ((), (), s32[]{:S(2)}) async-start(), calls=%async_computation.4 | async-start | bytes 4456448 | tf_op jit(solution)/shard_map/all_gather | solution.py:117
  337.6 123.5 %reduce-scatter.15.cloned.1.call-start = ((), (), s32[]{:S(2)}) async-start(), calls=%async_computation.9 | async-start | bytes 5242880
  415.4 0.9 copy-start.3
  415.4 95.9 %all-reduce.7.cloned.1.call-start = ((), (), s32[]{:S(2)}) async-start(), calls=%async_computation.5 | async-start | bytes 262144 | tf_op jit(solution)/shard_map/psum | solution.py:144
  438.3 73.1 %copy-start.5 = (bf16[16,2,32,128]{3,2,1,0:T(8,128)(2,1)S(1)}, bf16[16,2,32,128]{3,2,1,0:T(8,128)(2,1)}, u32[]{:S(2)}) copy-start(bf16[16,2,32,128]{3,2,1,0:T(8,128)(2,1)} %get-tuple-element.217) | copy-start | bytes 786436
Sparse Core Ops, SparseCore 0:
  41.4 73.4 reduce-scatter.10
  129.6 69.2 reduce-scatter.12
  200.8 31.1 all-gather.8
  240.2 48.1 all-reduce.8
  290.1 43.7 all-gather.4
  337.7 40.6 all-gather.6
  415.5 45.4 reduce-scatter.14
  464.0 47.2 all-reduce.6
where the time goes:
time: 521 us; the launch traced here: 520 us
  waiting for transfers between devices  376 us (72%)
  other arithmetic  44.7 us (9%)
  matrix products  37.7 us (7%)
  local copies, waits for them, and re-layouts  29.6 us (6%)
  blocking collectives  17.6 us (3%)
  between operations  14.3 us (3%)
    reduce_scatter x1, waiting for transfers between devices, local(): lax.psum_scatter(lax.dot_general(columns, depth_rows, (((0,), (1,)), ((),...  73.4 us
    reduce_scatter x1, waiting for transfers between devices, local(): lax.psum_scatter(lax.dot_general(columns, branch_act, (((0,), (0,)), ((),...  69.4 us
    psum x1, waiting for transfers between devices, spread(): return lax.psum(kept, axis)  48.3 us
    psum x1, waiting for transfers between devices, local(): lax.psum((kernel_grad, weight_grad * scaling, pw_bias_grad, proj_grad * s...  47.9 us
    all_gather x1, waiting for transfers between devices, local(): shard_rows = lax.all_gather(out_grad, 'chan', axis=0, tiled=True)  45.4 us
    all_gather x1, waiting for transfers between devices, local(): shard_rows = lax.all_gather(pre_grad, 'chan', axis=0, tiled=True)  40.8 us
    all_gather x1, waiting for transfers between devices, prefix(): everything = lax.all_gather(shard, axis)  32.1 us
    unnamed x29, local copies, waits for them, and re-layouts  29.6 us
  transfers between devices with their start and end apart: 8, of which 8 were waited for; matrix products, arithmetic and copies ran while one was open for 2% of the time, Pallas kernels for 0%

commit v1 on v0

--- a/solution.py
+++ b/solution.py
@@ -105,7 +105,9 @@
         spread(out_grad, "section", segments - 1),
     )
     proj_bias_grad = jnp.sum(out_grad.astype(jnp.float32), axis=1) * scaling
-    shard_rows = lax.all_gather(out_grad, "chan", axis=0, tiled=True)
+    shard_rows = jnp.concatenate(
+        lax.all_to_all(jnp.stack([out_grad] * lax.axis_size("chan")), "chan", 0, 0), axis=0
+    )
     act_grad = jnp.dot(proj_local, shard_rows, preferred_element_type=jnp.float32)
     piece_grad = lax.dot_general(
         branch_act, shard_rows, (((1,), (1,)), ((), ())), preferred_element_type=jnp.float32

time: 521 us -> 579 us (1.11)
  blocking collectives: 17.6 us -> 119 us
  waiting for transfers between devices: 376 us -> 330 us
    all_to_all x0 -> x1, blocking collectives: none -> 102 us  [local(): lax.all_to_all(jnp.stack([out_grad] * lax.axis_size('chan')), 'chan', 0, 0)]
    all_gather x1 -> x0, waiting for transfers between devices: 45.4 us -> none  [local(): shard_rows = lax.all_gather(out_grad, 'chan', axis=0, tiled=True)]
    unnamed x29 -> x33, local copies, waits for them, and re-layouts: 29.6 us -> 31.5 us
    unnamed x9 -> x8, waiting for transfers between devices: 18.4 us -> 18.4 us
  transfers between devices with their start and end apart: 8 -> 7, of which waited for: 8 -> 7; matrix products, arithmetic and copies ran while one was open for 2% -> 2% of each run, Pallas kernels for 0% -> 0%
where the time goes in v1:
time: 579 us; the launch traced here: 578 us
  waiting for transfers between devices  330 us (57%)
  blocking collectives  119 us (21%)
  other arithmetic  44.5 us (8%)
  matrix products  35.6 us (6%)
  local copies, waits for them, and re-layouts  33 us (6%)
  between operations  14.3 us (2%)
    all_to_all x1, blocking collectives, local(): lax.all_to_all(jnp.stack([out_grad] * lax.axis_size('chan')), 'chan', 0, 0)  102 us
    reduce_scatter x1, waiting for transfers between devices, local(): lax.psum_scatter(lax.dot_general(columns, depth_rows, (((0,), (1,)), ((),...  73.4 us
    reduce_scatter x1, waiting for transfers between devices, local(): lax.psum_scatter(lax.dot_general(columns, branch_act, (((0,), (0,)), ((),...  69.4 us
    psum x1, waiting for transfers between devices, spread(): return lax.psum(kept, axis)  48.3 us
    psum x1, waiting for transfers between devices, local(): lax.psum((kernel_grad, weight_grad * scaling, pw_bias_grad, proj_grad * s...  47.9 us
    all_gather x1, waiting for transfers between devices, local(): shard_rows = lax.all_gather(pre_grad, 'chan', axis=0, tiled=True)  40.9 us
    all_gather x1, waiting for transfers between devices, prefix(): everything = lax.all_gather(shard, axis)  32.1 us
    unnamed x33, local copies, waits for them, and re-layouts  31.5 us
  transfers between devices with their start and end apart: 7, of which 7 were waited for; matrix products, arithmetic and copies ran while one was open for 2% of the time, Pallas kernels for 0%

profile of v1, /device:TPU:2, one launch (start us, length us, event | category | flops | bytes accessed | tf_op | source)
XLA Modules:
  0.0 577.9 jit_solution(3494260360236183728)
XLA Ops:
  7.2 0.0 copy-start
  7.2 0.0 reduce-scatter.11.cloned.1.call-start
  7.2 0.7 convert_element_type.135
  7.9 0.7 fusion.36
  8.7 1.8 broadcast_multiply_fusion
  10.5 1.3 copy-done.2
  11.8 16.0 %fusion.10 = bf16[2,32,128,128]{3,2,1,0:T(8,128)(2,1)S(1)} fusion(bf16[2,32,128,128]{3,2,1,0:T(8,128)(2,1)S(1)} %broadcast_multiply_fusion, f32[128]{0:T(128)S(1)} %get-tuple-element.153, f32[128]{0:T(128)S(1)} %get-tuple-element.154, f32[128]{0:T(128)S(1)} %get-tuple-element.155, f32[128]{0:T(128)S(1)} %get-tuple-element.156, ...), kind=kLoop, calls=%fused_computation.50 | loop fusion | flops 28311552 | bytes 4198928 | tf_op jit(solution)/shard_map/convert_element_type | solution.py:69
  27.8 0.0 copy-done
  27.8 4.5 convolution_bitcast_fusion.1
  32.3 8.9 %copy.35 = f32[256,8192]{1,0:T(8,128)} copy(f32[256,8192]{0,1:T(8,128)} %convolution_bitcast_fusion.1) | data formatting | bytes 16777216
  41.2 0.0 reduce-scatter.11.cloned.1.call-update
  41.2 0.2 reduce-scatter.13.cloned.1.call-start
  41.5 73.4 %reduce-scatter.11.cloned.1.call-done = f32[16,8192]{1,0:T(8,128)} async-done(((f32[256,8192]{1,0:T(8,128)}), f32[16,8192]{1,0:T(8,128)}) %reduce-scatter.11.cloned.1.call-update) | async-done | bytes 524304 | tf_op jit(solution)/shard_map/reduce_scatter | solution.py:75
  114.9 0.0 copy-done.10
  114.9 5.6 convolution_bitcast_fusion
  120.6 8.9 %copy.37 = f32[256,8192]{1,0:T(8,128)} copy(f32[256,8192]{0,1:T(8,128)} %convolution_bitcast_fusion) | data formatting | bytes 16777216
  129.5 0.0 reduce-scatter.13.cloned.1.call-update
  129.5 0.0 all-gather.6.cloned.1.call-start
  129.6 69.4 %reduce-scatter.13.cloned.1.call-done = f32[16,8192]{1,0:T(8,128)} async-done(((f32[256,8192]{1,0:T(8,128)}), f32[16,8192]{1,0:T(8,128)}) %reduce-scatter.13.cloned.1.call-update) | async-done | bytes 524304 | tf_op jit(solution)/shard_map/reduce_scatter | solution.py:88
  198.9 0.0 all-gather.6.cloned.1.call-update
  199.0 0.0 all-reduce.9.cloned.1.call-start
  199.0 0.0 copy-done.6
  199.0 0.8 convert.2
  199.9 32.1 %all-gather.6.cloned.1.call-done = f32[64,8192]{1,0:T(8,128)} async-done(((f32[16,8192]{1,0:T(8,128)}), f32[64,8192]{1,0:T(8,128)}) %all-gather.6.cloned.1.call-update) | async-done | bytes 2097168 | tf_op jit(solution)/shard_map/all_gather | solution.py:13
  232.0 4.9 while.14
  232.0 1.2 add_select_fusion.2
  233.2 1.2 add_select_fusion.2
  234.4 1.2 add_select_fusion.2
  235.7 1.2 add_select_fusion.2
  236.9 0.0 copy-done.4
  236.9 0.0 copy-done.11
  236.9 2.2 broadcast_select_fusion
  239.1 0.8 copy.41
  239.9 0.0 all-reduce.9.cloned.1.call-update
  239.9 0.0 all-gather.4.cloned.1.call-start
  239.9 48.3 %all-reduce.9.cloned.1.call-done = (bf16[16,2,32,128]{3,2,1,0:T(8,128)(2,1)}, bf16[16,8192]{1,0:T(8,128)(2,1)}) async-done(((bf16[16,2,32,128]{3,2,1,0:T(8,128)(2,1)}, bf16[16,8192]{1,0:T(8,128)(2,1)}), (bf16[16,2,32,128]{3,2,1,0:T(8,128)(2,1)}, bf16[16,8192]{1,0:T(8,128)(2,1)})) %all-reduce.9.cloned.1.call-update) | async-done | bytes 524304 | tf_op jit(solution)/shard_map/psum | solution.py:26
  288.2 1.4 stack.4
  289.6 0.0 copy-start.3
  289.6 101.7 %all_to_all.5 = bf16[16,16,8192]{2,1,0:T(8,128)(2,1)S(1)} all-to-all(bf16[16,16,8192]{2,1,0:T(8,128)(2,1)S(1)} %stack.4), channel_id=1, replica_groups=mesh['section'=4,'dp'=4,'chan'=16] {'chan'}, dimensions={0} | all-to-all | bytes 8388608 | tf_op jit(solution)/shard_map/all_to_all | solution.py:109
  391.4 1.9 copy-done.1
  393.3 1.5 convert_reduce_fusion.1
  394.8 0.0 all-gather.4.cloned.1.call-update
  394.8 0.0 reduce-scatter.15.cloned.1.call-start
  394.9 40.9 %all-gather.4.cloned.1.call-done = bf16[256,8192]{1,0:T(8,128)(2,1)} async-done(((bf16[16,8192]{1,0:T(8,128)(2,1)}), bf16[256,8192]{1,0:T(8,128)(2,1)}) %all-gather.4.cloned.1.call-update) | async-done | bytes 4194320 | tf_op jit(solution)/shard_map/all_gather | solution.py:119
  435.8 16.1 %fusion.24 = (f32[128]{0:T(128)S(1)}, f32[128]{0:T(128)S(1)}, f32[128]{0:T(128)S(1)}, f32[128]{0:T(128)S(1)}, f32[128]{0:T(128)S(1)}, /*index=5*/f32[128]{0:T(12...) fusion(s32[]{:T(128)S(6)} %select_n.96, s32[]{:T(128)S(6)} %select_n.95, ...), kind=kOutput, calls=%fused_computation.64 | convolution fusion | flops 567278464 | bytes 8458768 | tf_op jit(solution)/shard_map/dot_general | solution.py:121
  451.9 16.2 %fusion.15 = f32[2,32,128,128]{3,2,1,0:T(8,128)S(1)} fusion(bf16[2,32,128,128]{3,2,1,0:T(8,128)(2,1)S(1)} %bitcast.130, s32[]{:T(128)S(6)} %select_n.96, s32[]{:T(128)S(6)} %select_n.95, s32[]{:T(128)S(6)} %select_n.94, s32[]{:T(128)S(6)} %select_n.93, f32[128]{0:T(128)S(1)} %get-tuple-element.153, f32[128]{0:T(128)S(1)} %get-tuple-element.154, ...), kind=kLoop, calls=%fused_computation.55 | loop fusion | flops 27262976 | bytes 6296080 | tf_op jit(solution)/shard_map/add | solution.py:140
  468.1 0.3 copy.39
  468.4 4.4 copy.52
  472.8 0.0 reduce-scatter.15.cloned.1.call-update
  472.8 0.3 all-reduce.7.cloned.1.call-start
  473.1 0.6 copy-done.5
  473.7 0.2 convert_reduce_fusion
  473.9 3.4 fusion.26
  477.4 17.6 %all-reduce.2 = (f32[1,9,128]{2,1,0:T(8,128)S(1)}, f32[1,16]{1,0:T(1,128)}, f32[1,16,256]{2,1,0:T(8,128)}, f32[16]{0:T(128)}) all-reduce(f32[1,9,128]{2,1,0:T(8,128)S(1)} %bitcast.135, f32[1,16]{1,0:T(1,128)S(1)} %multiply_bitcast_fusion, f32[1,16,256]{2,1,0:T(8,128)S(1)} %fusion.26, ...), channel_id=1, replica_groups=mesh['section'=4,'dp'=4,'chan'=16] {'dp'}, use_global_device_ids=true, to_apply=%region_16.17 | all-reduce | flops 5280 | bytes 42240 | tf_op jit(solution)/shard_map/psum | solution.py:146
  495.1 0.6 copy.34
  495.6 4.5 fusion.25
  500.1 0.0 all-reduce.7.cloned.1.call-update
  500.2 18.3 %reduce-scatter.15.cloned.1.call-done = f32[8,32768]{1,0:T(8,128)} async-done(((f32[32,32768]{1,0:T(8,128)}), f32[8,32768]{1,0:T(8,128)}) %reduce-scatter.15.cloned.1.call-update) | async-done | bytes 1048592
  518.4 1.4 copy.44
  519.9 1.0 fusion.27
  520.8 47.9 %all-reduce.7.cloned.1.call-done = f32[1,128,256]{2,1,0:T(8,128)} async-done(((f32[1,128,256]{2,1,0:T(8,128)}), f32[1,128,256]{2,1,0:T(8,128)}) %all-reduce.7.cloned.1.call-update) | async-done | bytes 131088 | tf_op jit(solution)/shard_map/psum | solution.py:146
  568.7 0.0 copy-done.7
  568.7 0.7 copy.62
  569.4 1.6 copy.63
  (24 shorter events, 0.1 us)
Async XLA Ops:
  7.2 20.7 %copy-start = (bf16[1,128,256]{2,1,0:T(8,128)(2,1)S(1)}, bf16[1,128,256]{2,1,0:T(8,128)(2,1)}, u32[]{:S(2)}) copy-start(bf16[1,128,256]{2,1,0:T(8,128)(2,1)} %param.17) | copy-start | bytes 196612
  7.2 107.7 %reduce-scatter.11.cloned.1.call-start = ((), (), s32[]{:S(2)}) async-start(), calls=%async_computation.7 | async-start | bytes 8912896 | tf_op jit(solution)/shard_map/reduce_scatter | solution.py:75
  10.5 1.4 copy-start.2
  41.2 73.7 %copy-start.9 = (bf16[1,16,256]{2,1,0:T(8,128)(2,1)S(1)}, bf16[1,16,256]{2,1,0:T(8,128)(2,1)}, u32[]{:S(2)}) copy-start(bf16[1,16,256]{2,1,0:T(8,128)(2,1)} %param.19) | copy-start | bytes 24580
  41.2 73.7 %copy-start.10 = (f32[1,16]{1,0:T(1,128)S(1)}, f32[1,16]{1,0:T(1,128)}, u32[]{:S(2)}) copy-start(f32[1,16]{1,0:T(1,128)} %param.18) | copy-start | bytes 196
  41.2 157.7 %reduce-scatter.13.cloned.1.call-start = ((), (), s32[]{:S(2)}) async-start(), calls=%async_computation.8 | async-start | bytes 8912896 | tf_op jit(solution)/shard_map/reduce_scatter | solution.py:88
  129.5 69.5 %copy-start.6 = (bf16[16,2,32,128]{3,2,1,0:T(8,128)(2,1)S(1)}, bf16[16,2,32,128]{3,2,1,0:T(8,128)(2,1)}, u32[]{:S(2)}) copy-start(bf16[16,2,32,128]{3,2,1,0:T(8,128)(2,1)} %param.21) | copy-start | bytes 786436
  129.5 70.4 %copy-start.8 = (s32[2,32,128]{2,1,0:T(8,128)S(1)}, s32[2,32,128]{2,1,0:T(8,128)}, u32[]{:S(2)}) copy-start(s32[2,32,128]{2,1,0:T(8,128)} %param.15) | copy-start | bytes 98308
  129.5 102.5 %all-gather.6.cloned.1.call-start = ((), (), s32[]{:S(2)}) async-start(), calls=%async_computation.6 | async-start | bytes 2621440 | tf_op jit(solution)/shard_map/all_gather | solution.py:13
  199.0 89.3 %all-reduce.9.cloned.1.call-start = ((), (), s32[]{:S(2)}) async-start(), calls=%async_computation.10 | async-start | bytes 1048576 | tf_op jit(solution)/shard_map/psum | solution.py:26
  199.9 37.0 %copy-start.4 = (f32[16,8192]{1,0:T(8,128)S(1)}, f32[16,8192]{1,0:T(8,128)}, u32[]{:S(2)}) copy-start(f32[16,8192]{1,0:T(8,128)} %reduce-scatter.13.cloned.1.call-done) | copy-start | bytes 1572868
  199.9 37.0 %copy-start.11 = (f32[16]{0:T(128)S(1)}, f32[16]{0:T(128)}, u32[]{:S(2)}) copy-start(f32[16]{0:T(128)} %param.20) | copy-start | bytes 196
  239.9 195.9 %all-gather.4.cloned.1.call-start = ((), (), s32[]{:S(2)}) async-start(), calls=%async_computation.4 | async-start | bytes 4456448 | tf_op jit(solution)/shard_map/all_gather | solution.py:119
  289.6 103.7 %copy-start.3 = (f32[16,8192]{1,0:T(8,128)S(1)}, f32[16,8192]{1,0:T(8,128)}, u32[]{:S(2)}) copy-start(f32[16,8192]{1,0:T(8,128)} %reduce-scatter.11.cloned.1.call-done) | copy-start | bytes 1572868
  391.4 1.9 copy-start.1
  394.8 123.6 %reduce-scatter.15.cloned.1.call-start = ((), (), s32[]{:S(2)}) async-start(), calls=%async_computation.9 | async-start | bytes 5242880
  472.8 0.9 copy-start.5
  472.8 95.9 %all-reduce.7.cloned.1.call-start = ((), (), s32[]{:S(2)}) async-start(), calls=%async_computation.5 | async-start | bytes 262144 | tf_op jit(solution)/shard_map/psum | solution.py:146
  495.6 73.1 %copy-start.7 = (bf16[16,2,32,128]{3,2,1,0:T(8,128)(2,1)S(1)}, bf16[16,2,32,128]{3,2,1,0:T(8,128)(2,1)}, u32[]{:S(2)}) copy-start(bf16[16,2,32,128]{3,2,1,0:T(8,128)(2,1)} %get-tuple-element.217) | copy-start | bytes 786436
Sparse Core Ops, SparseCore 0:
  41.4 73.4 reduce-scatter.10
  129.6 69.2 reduce-scatter.12
  200.8 31.1 all-gather.5
  240.0 48.1 all-reduce.8
  394.9 40.8 all-gather.3
  472.9 45.4 reduce-scatter.14
  521.4 47.2 all-reduce.6
